TPU v7x, 32 devices: a whole 2x2x4 slice. The times are simulated.
32 devices in a mesh: sect: 2 (over core), lang: 4 (over z), mp: 4 (over y, x).
Axes of the slice: x: 2, y: 2, z: 4, core: 2. Of those that a mesh axis runs over, the one named last changes fastest.
Arguments:
- memory: bfloat16 [4, 2, 128, 4096], P('lang', None, None, ('sect', 'mp')), may hold values from -6 to 6
- queries: bfloat16 [4, 4, 128, 3072], P('lang', 'sect', None, 'mp'), may hold values from -6 to 6
- out_grad: bfloat16 [4, 4, 128, 3072], P('lang', 'sect', None, 'mp'), may hold values from -6 to 6
- key_weight: bfloat16 [4, 4096, 3072], P('lang', None, 'mp'), may hold values from -0.09375 to 0.09375
- value_weight: bfloat16 [4, 4096, 3072], P('lang', None, 'mp'), may hold values from -0.09375 to 0.09375
- lang_rows: int32 [4, 4], P('lang'), may hold values from 0 to 128, as said below
- group_of_lang: int32 [4], replicated, may hold values from 0 to 3, each once
- src_len: int32 [4, 2], P('lang'), may hold values from 16 to 128
Outputs:
- mem_grad: bfloat16 [4, 2, 128, 4096], P('lang', None, None, ('sect', 'mp'))
Inputs may be any that keep to these rules, and one draw needn't show every extreme that they name: `lang_rows`: each entry is 0 or 128; each row has exactly 2 nonzero entries.
All inputs are finite; a program needn't handle non-finite values.
Results may differ from a plain program's by a relative error of at most 0.013.
Values may be sent and summed in bfloat16 or wider, within the bound.
A program may use at most 128 MiB of HBM per device.

v0:
```python
import jax
import jax.numpy as jnp
from jax import lax
from jax.sharding import PartitionSpec as P

HD = 128


def key_grads(key_rows, value_rows, queries, out_grad, lengths, head_dim):
    slots, source, width = key_rows.shape
    target = queries.shape[1]
    heads = width // head_dim
    key_four = key_rows.reshape(slots, source, heads, head_dim)
    value_four = value_rows.reshape(slots, source, heads, head_dim)
    query_four = queries.reshape(slots, target, heads, head_dim)
    grad_four = out_grad.reshape(slots, target, heads, head_dim)
    scaling = head_dim ** (-0.5)
    score_table = (
        jnp.einsum("sqhd,skhd->shqk", query_four, key_four, preferred_element_type=jnp.float32)
        * scaling
    )
    visible = jnp.arange(source, dtype=jnp.int32)[None, :] < lengths[:, None]
    weights = jnp.where(visible[:, None, None, :], jnp.exp(score_table), 0.0)
    probs = weights / jnp.sum(weights, axis=-1, keepdims=True)
    probs_low = probs.astype(jnp.bfloat16)
    grad_probs = jnp.einsum(
        "sqhd,skhd->shqk", grad_four, value_four, preferred_element_type=jnp.float32
    )
    deltas = jnp.sum(probs * grad_probs, axis=-1, keepdims=True)
    grad_scores = (probs * (grad_probs - deltas) * scaling).astype(jnp.bfloat16)
    grad_keys = jnp.einsum(
        "shqk,sqhd->skhd", grad_scores, query_four, preferred_element_type=jnp.float32
    )
    grad_values = jnp.einsum(
        "shqk,sqhd->skhd", probs_low, grad_four, preferred_element_type=jnp.float32
    )
    grad_keys = grad_keys.astype(jnp.bfloat16).reshape(slots, source, width)
    grad_values = grad_values.astype(jnp.bfloat16).reshape(slots, source, width)
    return (grad_keys, grad_values)


def back_project(grad_keys, grad_values, key_cols, value_cols):
    contract = (((1,), (1,)), ((), ()))
    flat_keys = grad_keys.reshape(-1, grad_keys.shape[2])
    flat_values = grad_values.reshape(-1, grad_values.shape[2])
    term = lax.dot_general(flat_keys, key_cols, contract, preferred_element_type=jnp.float32)
    return term + lax.dot_general(
        flat_values, value_cols, contract, preferred_element_type=jnp.float32
    )


def body(memory, queries, out_grad, key_weight, value_weight, lang_rows, group_of_lang, src_len):
    blocks = memory.shape[1]
    source = memory.shape[2]
    eighth = memory.shape[3]
    width = key_weight.shape[1]
    head_cols = key_weight.shape[2]
    groups = lax.axis_size("lang")
    sectors = lax.axis_size("sect")
    quarters = lax.axis_size("mp")
    sector = lax.axis_index("sect")
    per_half = groups // sectors
    is_live = (lang_rows[0] > 0).astype(jnp.int32)
    ranking = jnp.cumsum(is_live) - 1
    block_index = jnp.arange(blocks, dtype=jnp.int32)
    chosen = (is_live[None, :] > 0) & (ranking[None, :] == block_index[:, None])
    block_group = jnp.sum(jnp.where(chosen, group_of_lang[None, :], 0), axis=1)
    routing = block_group[None, :] == jnp.arange(groups, dtype=jnp.int32)[:, None]
    outgoing = jnp.dot(
        routing.astype(jnp.bfloat16),
        memory[0].reshape(blocks, source * eighth),
        preferred_element_type=jnp.float32,
    )
    outgoing = outgoing.astype(jnp.bfloat16).reshape(groups, source, eighth)
    sent_len = jnp.sum(jnp.where(routing, src_len[0][None, :], 0), axis=1)[:, None]
    panels, got_len = (
        lax.all_to_all(outgoing, "lang", split_axis=0, concat_axis=0, tiled=True),
        lax.all_to_all(sent_len, "lang", split_axis=0, concat_axis=0, tiled=True),
    )
    lengths_all = jnp.maximum(got_len[:, 0], 1)
    halves = lax.all_gather(panels, "mp", axis=2, tiled=True)
    full_rows = lax.all_to_all(halves, "sect", split_axis=0, concat_axis=2, tiled=True).reshape(
        per_half * source, width
    )
    key_rows = jnp.dot(full_rows, key_weight[0], preferred_element_type=jnp.float32).astype(
        jnp.bfloat16
    )
    value_rows = jnp.dot(full_rows, value_weight[0], preferred_element_type=jnp.float32).astype(
        jnp.bfloat16
    )
    lengths = lax.dynamic_slice_in_dim(lengths_all, sector * per_half, per_half)
    grad_keys, grad_values = key_grads(
        key_rows.reshape(per_half, source, head_cols),
        value_rows.reshape(per_half, source, head_cols),
        queries[0],
        out_grad[0],
        lengths,
        HD,
    )
    partial_value = back_project(grad_keys, grad_values, key_weight[0], value_weight[0])
    term = partial_value.reshape(per_half, source, sectors, quarters, eighth)
    summed = lax.psum_scatter(term.astype(jnp.bfloat16), "mp", scatter_dimension=3, tiled=True)
    returned = lax.all_to_all(summed, "sect", split_axis=2, concat_axis=0, tiled=True).reshape(
        groups, source, eighth
    )
    arrived = lax.all_to_all(returned, "lang", split_axis=0, concat_axis=0, tiled=True)
    picked = jnp.dot(
        routing.T.astype(jnp.bfloat16),
        arrived.reshape(groups, source * eighth),
        preferred_element_type=jnp.float32,
    )
    return picked.astype(jnp.bfloat16).reshape(1, blocks, source, eighth)


def solution(mesh):
    in_specs = (
        P("lang", None, None, ("sect", "mp")),
        P("lang", "sect", None, "mp"),
        P("lang", "sect", None, "mp"),
        P("lang", None, "mp"),
        P("lang", None, "mp"),
        P("lang", None),
        P(),
        P("lang", None),
    )
    out_specs = P("lang", None, None, ("sect", "mp"))
    return jax.shard_map(body, mesh=mesh, in_specs=in_specs, out_specs=out_specs, check_vma=False)
```

profile of v0, /device:TPU:1, one launch (start us, length us, event | category | flops | bytes accessed | tf_op | source)
XLA Modules:
  0.0 208.6 jit_solution(2022954227562717644)
XLA Ops:
  7.5 1.2 copy.114
  8.7 0.8 fusion.44
  10.1 19.0 %all_to_all.49 = bf16[4,128,512]{2,1,0:T(8,128)(2,1)} all-to-all(bf16[4,128,512]{2,1,0:T(8,128)(2,1)S(1)} %bitcast.103), channel_id=1, replica_groups=mesh['sect'=2,'lang'=4,'mp'=4] {'lang'}, dimensions={0} | all-to-all | bytes 1048576 | tf_op jit(solution)/shard_map/all_to_all | solution.py:77
  30.6 3.2 %all-to-all-start = ((s32[4,1,1]{2,1,0:T(1,128)}), s32[4,1,1]{2,1,0:T(1,128)S(1)}, u32[]{:S(2)}, u32[]{:S(2)}) async-start(s32[4,1,1]{2,1,0:T(1,128)} %copy.85), calls=%async_computation | async-start | bytes 4096 | tf_op jit(solution)/shard_map/all_to_all | solution.py:78
  33.9 0.9 copy.88
  35.0 3.1 %all-to-all-done = s32[4,1,1]{2,1,0:T(1,128)S(1)} async-done(((s32[4,1,1]{2,1,0:T(1,128)}), s32[4,1,1]{2,1,0:T(1,128)S(1)}, u32[]{:S(2)}, u32[]{:S(2)}) %all-to-all-start) | async-done | bytes 48 | tf_op jit(solution)/shard_map/all_to_all | solution.py:78
  38.3 26.1 %all-gather.2.cloned.1.call-done = bf16[4,128,2048]{2,1,0:T(8,128)(2,1)} async-done(((bf16[4,128,512]{2,1,0:T(8,128)(2,1)}), bf16[4,128,2048]{2,1,0:T(8,128)(2,1)}) %all-gather.2.cloned.1.call-update) | async-done | bytes 2097168 | tf_op jit(solution)/shard_map/all_gather | solution.py:81
  64.4 7.3 %all_to_all.50 = bf16[4,128,2048]{2,1,0:T(8,128)(2,1)S(1)} all-to-all(bf16[4,128,2048]{2,1,0:T(8,128)(2,1)} %all-gather.2.cloned.1.call-done), channel_id=1, replica_groups=mesh['sect'=2,'lang'=4,'mp'=4] {'sect'}, dimensions={0} | all-to-all | bytes 4194304 | tf_op jit(solution)/shard_map/all_to_all | solution.py:82
  71.8 2.2 %copy.86 = bf16[2,128,2,2048]{3,2,1,0:T(2,128)(2,1)S(1)} copy(bf16[2,128,2,2048]{3,1,0,2:T(8,128)(2,1)S(1)} %bitcast.97) | data formatting | bytes 4194304 | tf_op jit(solution)/shard_map/all_to_all | solution.py:82
  73.9 0.9 copy.116
  74.8 1.9 fusion.24
  77.2 2.3 %fusion.42 = f32[2,6,128,128]{2,3,1,0:T(8,128)} fusion(bf16[2,128,6,128]{1,3,2,0:T(8,128)(2,1)} %bitcast.112, bf16[2,128,6,128]{3,2,1,0:T(8,128)(2,1)S(1)} %reshape.84, pred[2,128]{1,0:T(4,128)(4,1)S(1)} %iota_compare_fusion), kind=kOutput, calls=%fused_computation.41 | convolution fusion | flops 50923136 | bytes 1573120 | tf_op jit(solution)/shard_map/div | solution.py:24
  79.5 1.2 fusion.18
  80.7 4.6 %fusion.27 = bf16[256,768]{1,0:T(8,128)(2,1)S(1)} fusion(bf16[256,4096]{1,0:T(8,128)(2,1)S(1)} %bitcast.102, bf16[1,4096,768]{2,1,0:T(8,128)(2,1)} %param.12), kind=kOutput, calls=%fused_computation.26 | convolution fusion | flops 1610809344 | bytes 8781824 | tf_op jit(solution)/shard_map/dot_general | solution.py:88
  86.0 1.8 fusion.31
  88.1 1.8 fusion.30
  90.5 4.6 %fusion.1 = f32[256,4096]{1,0:T(8,128)S(1)} fusion(bf16[1,4096,768]{2,1,0:T(8,128)(2,1)} %param.12, bf16[96,8,2,128]{3,2,1,0:T(2,128)(2,1)S(1)} %bitcast.115), kind=kOutput, calls=%fused_computation.3 | convolution fusion | flops 1610612736 | bytes 10878976 | tf_op jit(solution)/shard_map/dot_general | solution.py:47
  95.2 4.6 %fusion.12 = bf16[256,4096]{1,0:T(8,128)(2,1)S(1)} fusion(f32[256,4096]{1,0:T(8,128)S(1)} %fusion.1, bf16[1,4096,768]{2,1,0:T(8,128)(2,1)} %param.11, bf16[96,8,2,128]{3,2,1,0:T(2,128)(2,1)S(1)} %bitcast.107), kind=kOutput, calls=%fused_computation.12 | convolution fusion | flops 1612709888 | bytes 12976128 | tf_op jit(solution)/shard_map/dot_general | solution.py:46
  99.8 2.8 %convert_element_type.57 = bf16[2,128,2,4,512]{4,3,2,1,0:T(4,128)(2,1)} reshape(bf16[256,4096]{1,0:T(8,128)(2,1)S(1)} %fusion.12) | data formatting | bytes 4194304 | tf_op jit(solution)/shard_map/convert_element_type | solution.py:102
  102.6 3.6 %copy.100 = bf16[2,128,2,4,512]{4,1,3,2,0:T(8,128)(2,1)} copy(bf16[2,128,2,4,512]{4,3,2,1,0:T(4,128)(2,1)} %convert_element_type.57) | data formatting | bytes 4194304 | tf_op jit(solution)/shard_map/convert_element_type | solution.py:102
  106.9 68.6 %all-reduce.3.cloned.1.call-done = bf16[2,128,2,4,512]{4,1,3,2,0:T(8,128)(2,1)} async-done(((bf16[2,128,2,4,512]{4,1,3,2,0:T(8,128)(2,1)}), bf16[2,128,2,4,512]{4,1,3,2,0:T(8,128)(2,1)}) %all-reduce.3.cloned.1.call-update) | async-done | bytes 2097168
  175.5 1.7 constant_dynamic-slice_fusion
  177.2 4.6 %all_to_all.51 = bf16[2,128,2,1,512]{4,1,3,0,2:T(8,128)(2,1)S(1)} all-to-all(bf16[2,128,2,1,512]{4,1,3,0,2:T(8,128)(2,1)S(1)} %copy.101), channel_id=1, replica_groups=mesh['sect'=2,'lang'=4,'mp'=4] {'sect'}, dimensions={2} | all-to-all | bytes 1048576 | tf_op jit(solution)/shard_map/all_to_all | solution.py:103
  181.9 18.2 %all_to_all.52 = bf16[4,128,512]{2,1,0:T(8,128)(2,1)S(1)} all-to-all(bf16[4,128,512]{2,1,0:T(8,128)(2,1)S(1)} %bitcast.105), channel_id=1, replica_groups=mesh['sect'=2,'lang'=4,'mp'=4] {'lang'}, dimensions={0} | all-to-all | bytes 1048576 | tf_op jit(solution)/shard_map/all_to_all | solution.py:106
  (39 shorter events, 8.0 us)
Async XLA Ops:
  6.5 27.3 %copy-start = (bf16[1,2,128,768]{3,2,1,0:T(8,128)(2,1)S(1)}, bf16[1,2,128,768]{3,2,1,0:T(8,128)(2,1)}, u32[]{:S(2)}) copy-start(bf16[1,2,128,768]{3,2,1,0:T(8,128)(2,1)} %param.9) | copy-start | bytes 1179652
  6.5 28.3 %copy-start.1 = (bf16[1,2,128,768]{3,2,1,0:T(8,128)(2,1)S(1)}, bf16[1,2,128,768]{3,2,1,0:T(8,128)(2,1)}, u32[]{:S(2)}) copy-start(bf16[1,2,128,768]{3,2,1,0:T(8,128)(2,1)} %param.10) | copy-start | bytes 1179652
  6.5 57.9 %all-gather.2.cloned.1.call-start = ((), (), s32[]{:S(2)}) async-start(), calls=%async_computation.5 | async-start | bytes 2621440 | tf_op jit(solution)/shard_map/all_gather | solution.py:81
  30.6 7.5 %all-to-all-start = ((s32[4,1,1]{2,1,0:T(1,128)}), s32[4,1,1]{2,1,0:T(1,128)S(1)}, u32[]{:S(2)}, u32[]{:S(2)}) async-start(s32[4,1,1]{2,1,0:T(1,128)} %copy.85), calls=%async_computation | async-start | bytes 4096 | tf_op jit(solution)/shard_map/all_to_all | solution.py:78
  33.8 141.6 %all-reduce.3.cloned.1.call-start = ((), (), s32[]{:S(2)}) async-start(), calls=%async_computation.6 | async-start | bytes 4194304
  64.4 10.4 %slice-start = ((s8[6291456]{0:T(1024)(128)(4,1)}), s8[4194304]{0:T(1024)(128)(4,1)S(1)}, s32[]{:S(2)}) async-start(s8[6291456]{0:T(1024)(128)(4,1)} %bitcast.99), calls=%async_computation.7 | async-start | bytes 8388608
  71.7 3.1 %slice-start.1 = ((s8[6291456]{0:T(1024)(128)(4,1)}), s8[2097152]{0:T(1024)(128)(4,1)S(1)}, s32[]{:S(2)}) async-start(s8[6291456]{0:T(1024)(128)(4,1)} %bitcast.99), calls=%async_computation.8 | async-start | bytes 4194304
  77.2 2.3 %copy-start.2 = (bf16[1,2,128,768]{2,3,1,0:T(8,128)(2,1)S(1)}, bf16[1,2,128,768]{2,3,1,0:T(8,128)(2,1)}, u32[]{:S(2)}) copy-start(bf16[1,2,128,768]{2,3,1,0:T(8,128)(2,1)} %copy.88) | copy-start | bytes 1179652
  102.6 3.7 %copy-start.3 = (u32[32]{0:T(128)S(1)}, u32[32]{0:T(128)}, u32[]{:S(2)}) copy-start(u32[32]{0:T(128)} %constant.35) | copy-start | bytes 388
Sparse Core Ops, SparseCore 0:
  29.3 35.0 all-gather.1
  106.4 69.0 all-reduce.2
where the time goes:
time: 211 us; the launch traced here: 209 us
  waiting for transfers between devices  97.8 us (46%)
  blocking collectives  49.1 us (23%)
  matrix products  24 us (11%)
  local copies, waits for them, and re-layouts  18.1 us (9%)
  between operations  13.6 us (6%)
  starting transfers between devices  3.27 us (2%)
  other arithmetic  2.63 us (1%)
    unnamed x3, waiting for transfers between devices  68.6 us
    all_gather x1, waiting for transfers between devices, body(): halves = lax.all_gather(panels, 'mp', axis=2, tiled=True)  26.1 us
    all_to_all x1, blocking collectives, body(): lax.all_to_all(outgoing, 'lang', split_axis=0, concat_axis=0, tiled=True)  19 us
    all_to_all x1, blocking collectives, body(): lax.all_to_all(returned, 'lang', split_axis=0, concat_axis=0, tiled=True)  18.2 us
    all_to_all x1, blocking collectives, body(): lax.all_to_all(halves, 'sect', split_axis=0, concat_axis=2, tiled=True)  7.34 us
    unnamed x21, local copies, waits for them, and re-layouts  6.81 us
    convert_element_type x2, local copies, waits for them, and re-layouts, body(): term.astype(jnp.bfloat16)  6.44 us
    dot_general x1, matrix products, back_project(): lax.dot_general(flat_keys, key_cols, contract, preferred_element_type=jnp...  4.64 us
  transfers between devices with their start and end apart: 3, of which 3 were waited for; matrix products, arithmetic and copies ran while one was open for 2% of the time, Pallas kernels for 0%

commit v1 on v0

v1 whole, which is shorter than its diff:
```python
import functools

import jax
import jax.numpy as jnp
from jax import lax
from jax.experimental import pallas as pl
from jax.experimental.pallas import tpu as pltpu
from jax.sharding import PartitionSpec as P

HD = 128
MESH = pl.DeviceIdType.MESH
NT = (((1,), (1,)), ((), ()))


def kernel(
    dims,
    lang_rows,
    group_of_lang,
    src_len,
    memory,
    queries_hbm,
    grads_hbm,
    key_hbm,
    value_hbm,
    out,
    key_w,
    value_w,
    query_v,
    grad_v,
    outgoing,
    out_len,
    got_len,
    rows,
    acc_k,
    acc_v,
    key_rows,
    value_rows,
    part,
    own,
    inbox,
    reduced,
    arrived,
    load_sem,
    z_send,
    z_len_send,
    len_recv,
    rows_recv,
    mp_send,
    part_send,
    part_recv,
    back_send,
    back_recv,
):
    sectors, groups, quarters, half, blocks, source, eighth, width, heads_w = dims
    ms, ml, mq = lax.axis_index("sect"), lax.axis_index("lang"), lax.axis_index("mp")
    languages = lang_rows.shape[1]

    loads = [
        pltpu.make_async_copy(key_hbm.at[0], key_w, load_sem.at[0]),
        pltpu.make_async_copy(value_hbm.at[0], value_w, load_sem.at[1]),
        pltpu.make_async_copy(queries_hbm.at[0], query_v, load_sem.at[2]),
        pltpu.make_async_copy(grads_hbm.at[0], grad_v, load_sem.at[3]),
    ]

    barrier = pltpu.get_barrier_semaphore()
    for ds in range(sectors):
        for dl in range(groups):
            if ds or dl:
                peer = (lax.rem(ms + ds, sectors), lax.rem(ml + dl, groups), mq)
                pl.semaphore_signal(barrier, inc=1, device_id=peer, device_id_type=MESH)
    for dq in range(1, quarters):
        peer = (ms, ml, lax.rem(mq + dq, quarters))
        pl.semaphore_signal(barrier, inc=1, device_id=peer, device_id_type=MESH)
    for load in loads:
        load.start()

    live, rank, count = [], [], 0
    for c in range(languages):
        live.append((lang_rows[0, c] > 0).astype(jnp.int32))
        rank.append(count)
        count = count + live[c]
    home = lax.div(ml, half)
    slot = lax.rem(ml, half)
    at_home = home == ms
    for dl in range(groups):
        g = lax.rem(ml + dl, groups)
        index, routed = 0, 0
        for c in range(languages):
            hit = jnp.where(group_of_lang[c] == g, live[c], 0)
            index = index + hit * rank[c]
            routed = routed + hit
        outgoing[dl] = memory[0, index]
        length = jnp.maximum(jnp.where(routed > 0, src_len[0, index], 1), 1)
        out_len[dl] = jnp.full(out_len.shape[1:], length, jnp.int32)

    pl.semaphore_wait(barrier, sectors * groups - 1 + quarters - 1)

    def z_copy(dl):
        g = lax.rem(ml + dl, groups)
        data = pltpu.make_async_remote_copy(
            src_ref=outgoing.at[dl],
            dst_ref=rows.at[ms, mq, slot],
            send_sem=z_send.at[dl],
            recv_sem=rows_recv.at[ms, mq, slot],
            device_id=(home, g, mq),
            device_id_type=MESH,
        )
        lens = pltpu.make_async_remote_copy(
            src_ref=out_len.at[dl],
            dst_ref=got_len.at[slot, ms],
            send_sem=z_len_send.at[dl],
            recv_sem=len_recv.at[slot, ms],
            device_id=(home, g, mq),
            device_id_type=MESH,
        )
        return data, lens

    def local_in():
        return (
            pltpu.make_async_copy(
                outgoing.at[0], rows.at[ms, mq, slot], rows_recv.at[ms, mq, slot]
            ),
            pltpu.make_async_copy(
                out_len.at[0], got_len.at[slot, ms], len_recv.at[slot, ms]
            ),
        )

    @pl.when(at_home)
    def _():
        for copy in local_in():
            copy.start()

    @pl.when(jnp.logical_not(at_home))
    def _():
        for copy in z_copy(0):
            copy.start()

    for dl in range(1, groups):
        for copy in z_copy(dl):
            copy.start()

    def landed(s, q, ls):
        view = rows.at[s, q, ls]
        pltpu.make_async_copy(view, view, rows_recv.at[s, q, ls]).wait()

    def mp_copy(s, ls, dq):
        return pltpu.make_async_remote_copy(
            src_ref=rows.at[s, mq, ls],
            dst_ref=rows.at[s, mq, ls],
            send_sem=mp_send.at[dq - 1, s, ls],
            recv_sem=rows_recv.at[s, mq, ls],
            device_id=(ms, ml, lax.rem(mq + dq, quarters)),
            device_id_type=MESH,
        )

    nearest = jnp.clip(ml - ms * half, 0, half - 1)

    def forward(i, carry):
        ls = lax.rem(nearest + lax.div(i, sectors), half)
        s = lax.rem(i, sectors)
        landed(s, mq, ls)
        for dq in range(quarters - 1, 0, -1):
            mp_copy(s, ls, dq).start()
        return carry

    lax.fori_loop(0, sectors * half, forward, 0)

    pair = 2 if half % 2 == 0 else 1
    tall = pair * source
    acc_k[...] = jnp.zeros_like(acc_k)
    acc_v[...] = jnp.zeros_like(acc_v)
    for load in loads:
        load.wait()

    def project(i, carry):
        q = lax.rem(mq + lax.div(i, sectors), quarters)
        s = lax.rem(i, sectors)

        @pl.when(q != mq)
        def _():
            def wait_slot(ls, c):
                landed(s, q, ls)
                return c

            lax.fori_loop(0, half, wait_slot, 0)

        start = pl.multiple_of((s * quarters + q) * eighth, eighth)

        def chunk(m, c):
            x = rows[s, q, pl.ds(m * pair, pair)].reshape(tall, eighth)
            at = pl.ds(pl.multiple_of(m * tall, tall), tall)
            acc_k[at, :] += jnp.dot(
                x, key_w[pl.ds(start, eighth), :], preferred_element_type=jnp.float32
            )
            acc_v[at, :] += jnp.dot(
                x, value_w[pl.ds(start, eighth), :], preferred_element_type=jnp.float32
            )
            return c

        return lax.fori_loop(0, half // pair, chunk, carry)

    lax.fori_loop(0, sectors * quarters, project, 0)

    def wait_len(i, carry):
        ls, s = lax.div(i, sectors), lax.rem(i, sectors)
        view = got_len.at[ls, s]
        pltpu.make_async_copy(view, view, len_recv.at[ls, s]).wait()
        return carry

    lax.fori_loop(0, sectors * half, wait_len, 0)

    scaling = HD ** (-0.5)
    position = lax.broadcasted_iota(jnp.int32, (source, query_v.shape[1]), 0)

    def attend(ls, carry):
        at = pl.ds(pl.multiple_of(ls * source, source), source)
        visible = position < got_len[ls, 0][0:1, :]
        for h in range(heads_w // HD):
            cols = slice(h * HD, (h + 1) * HD)
            k = acc_k[at, cols].astype(jnp.bfloat16)
            v = acc_v[at, cols].astype(jnp.bfloat16)
            q = query_v[ls, :, cols]
            d = grad_v[ls, :, cols]
            scores = lax.dot_general(k, q, NT, preferred_element_type=jnp.float32) * scaling
            weights = jnp.where(visible, jnp.exp(scores), 0.0)
            probs = weights / jnp.sum(weights, axis=0, keepdims=True)
            grad_probs = lax.dot_general(v, d, NT, preferred_element_type=jnp.float32)
            deltas = jnp.sum(probs * grad_probs, axis=0, keepdims=True)
            grad_scores = (probs * (grad_probs - deltas) * scaling).astype(jnp.bfloat16)
            key_rows[at, cols] = jnp.dot(
                grad_scores, q, preferred_element_type=jnp.float32
            ).astype(jnp.bfloat16)
            value_rows[at, cols] = jnp.dot(
                probs.astype(jnp.bfloat16), d, preferred_element_type=jnp.float32
            ).astype(jnp.bfloat16)
        return carry

    lax.fori_loop(0, half, attend, 0)

    def part_copy(s, ls, dq):
        q = lax.rem(mq + dq, quarters)
        return pltpu.make_async_remote_copy(
            src_ref=part.at[dq - 1, s, ls],
            dst_ref=inbox.at[dq - 1, s, ls],
            send_sem=part_send.at[dq - 1, s, ls],
            recv_sem=part_recv.at[dq - 1, s, ls],
            device_id=(ms, ml, q),
            device_id_type=MESH,
        )

    def project_back(s, q, m):
        start = pl.multiple_of((s * quarters + q) * eighth, eighth)
        at = pl.ds(pl.multiple_of(m * tall, tall), tall)
        term = lax.dot_general(
            key_rows[at, :], key_w[pl.ds(start, eighth), :], NT,
            preferred_element_type=jnp.float32,
        )
        return term + lax.dot_general(
            value_rows[at, :], value_w[pl.ds(start, eighth), :], NT,
            preferred_element_type=jnp.float32,
        )

    chunks = half // pair

    def send_part(i, carry):
        m = lax.rem(i, chunks)
        s = lax.rem(lax.div(i, chunks), sectors)
        dq = quarters - 1 - lax.div(i, chunks * sectors)
        term = project_back(s, lax.rem(mq + dq, quarters), m)
        part[dq - 1, s, pl.ds(m * pair, pair)] = term.astype(jnp.bfloat16).reshape(
            pair, source, eighth
        )
        for p in range(pair):
            part_copy(s, m * pair + p, dq).start()
        return carry

    lax.fori_loop(0, (quarters - 1) * sectors * chunks, send_part, 0)

    def keep_part(i, carry):
        m, s = lax.rem(i, chunks), lax.div(i, chunks)
        own[s, pl.ds(m * pair, pair)] = project_back(s, mq, m).reshape(pair, source, eighth)
        return carry

    lax.fori_loop(0, sectors * chunks, keep_part, 0)

    def back_copy(s, ls):
        return pltpu.make_async_remote_copy(
            src_ref=reduced.at[s, ls],
            dst_ref=arrived.at[ml],
            send_sem=back_send.at[s, ls],
            recv_sem=back_recv.at[ml],
            device_id=(s, ms * half + ls, mq),
            device_id_type=MESH,
        )

    def local_back(s, ls):
        return pltpu.make_async_copy(reduced.at[s, ls], arrived.at[ml], back_recv.at[ml])

    def is_me(s, ls):
        return jnp.logical_and(s == ms, ms * half + ls == ml)

    def reduce(i, carry):
        ls, s = lax.rem(i, half), lax.div(i, half)
        total = own[s, ls]
        for dq in range(quarters - 1, 0, -1):
            view = inbox.at[dq - 1, s, ls]
            pltpu.make_async_copy(view, view, part_recv.at[dq - 1, s, ls]).wait()
            total = total + inbox[dq - 1, s, ls].astype(jnp.float32)
        reduced[s, ls] = total.astype(jnp.bfloat16)

        @pl.when(is_me(s, ls))
        def _():
            local_back(s, ls).start()

        @pl.when(jnp.logical_not(is_me(s, ls)))
        def _():
            back_copy(s, ls).start()

        return carry

    lax.fori_loop(0, sectors * half, reduce, 0)

    for g in range(groups):
        view = arrived.at[g]
        pltpu.make_async_copy(view, view, back_recv.at[g]).wait()
    for j in range(blocks):
        group = 0
        for c in range(languages):
            group = group + jnp.where(rank[c] == j, live[c] * group_of_lang[c], 0)
        out[0, j] = arrived[group]

    @pl.when(jnp.logical_not(at_home))
    def _():
        for copy in z_copy(0):
            copy.wait_send()

    for dl in range(1, groups):
        for copy in z_copy(dl):
            copy.wait_send()

    def drain(i, carry):
        ls, s = lax.rem(i, half), lax.div(i, half)
        for dq in range(1, quarters):
            mp_copy(s, ls, dq).wait_send()
            part_copy(s, ls, dq).wait_send()

        @pl.when(jnp.logical_not(is_me(s, ls)))
        def _():
            back_copy(s, ls).wait_send()

        return carry

    lax.fori_loop(0, sectors * half, drain, 0)


def body(memory, queries, out_grad, key_weight, value_weight, lang_rows, group_of_lang, src_len):
    blocks, source, eighth = memory.shape[1:]
    width, heads_w = key_weight.shape[1:]
    sectors, groups = lax.axis_size("sect"), lax.axis_size("lang")
    quarters = lax.axis_size("mp")
    half = groups // sectors
    dims = (sectors, groups, quarters, half, blocks, source, eighth, width, heads_w)
    low, full = jnp.bfloat16, jnp.float32
    vmem = pl.BlockSpec(memory_space=pltpu.VMEM)
    smem = pl.BlockSpec(memory_space=pltpu.SMEM)
    hbm = pl.BlockSpec(memory_space=pl.ANY)
    dma = pltpu.SemaphoreType.DMA
    scratch = [
        pltpu.VMEM((width, heads_w), low),
        pltpu.VMEM((width, heads_w), low),
        pltpu.VMEM(queries.shape[1:], low),
        pltpu.VMEM(queries.shape[1:], low),
        pltpu.VMEM((groups, source, eighth), low),
        pltpu.VMEM((groups, 8, queries.shape[2]), jnp.int32),
        pltpu.VMEM((half, sectors, 8, queries.shape[2]), jnp.int32),
        pltpu.VMEM((sectors, quarters, half, source, eighth), low),
        pltpu.VMEM((half * source, heads_w), full),
        pltpu.VMEM((half * source, heads_w), full),
        pltpu.VMEM((half * source, heads_w), low),
        pltpu.VMEM((half * source, heads_w), low),
        pltpu.VMEM((quarters - 1, sectors, half, source, eighth), low),
        pltpu.VMEM((sectors, half, source, eighth), full),
        pltpu.VMEM((quarters - 1, sectors, half, source, eighth), low),
        pltpu.VMEM((sectors, half, source, eighth), low),
        pltpu.VMEM((groups, source, eighth), low),
        dma((4,)),
        dma((groups,)),
        dma((groups,)),
        dma((half, sectors)),
        dma((sectors, quarters, half)),
        dma((quarters - 1, sectors, half)),
        dma((quarters - 1, sectors, half)),
        dma((quarters - 1, sectors, half)),
        dma((sectors, half)),
        dma((groups,)),
    ]
    return pl.pallas_call(
        functools.partial(kernel, dims),
        out_shape=jax.ShapeDtypeStruct(memory.shape, memory.dtype),
        in_specs=[smem, smem, smem, vmem, hbm, hbm, hbm, hbm],
        out_specs=vmem,
        scratch_shapes=scratch,
        compiler_params=pltpu.CompilerParams(
            collective_id=0, has_side_effects=True, vmem_limit_bytes=67043328
        ),
    )(lang_rows, group_of_lang, src_len, memory, queries, out_grad, key_weight, value_weight)


def solution(mesh):
    in_specs = (
        P("lang", None, None, ("sect", "mp")),
        P("lang", "sect", None, "mp"),
        P("lang", "sect", None, "mp"),
        P("lang", None, "mp"),
        P("lang", None, "mp"),
        P("lang", None),
        P(),
        P("lang", None),
    )
    out_specs = P("lang", None, None, ("sect", "mp"))
    return jax.shard_map(body, mesh=mesh, in_specs=in_specs, out_specs=out_specs, check_vma=False)
```

time: 211 us -> 71.6 us (0.34); the launches traced: 209 us -> 71.5 us
  waiting for transfers between devices: 97.8 us -> 0 us
  Pallas kernels: 0 us -> 69.8 us
  blocking collectives: 49.1 us -> 0 us
  matrix products: 24 us -> 0 us
  local copies, waits for them, and re-layouts: 18.1 us -> 1.67 us
  between operations: 13.6 us -> 0.01 us
  starting transfers between devices: 3.27 us -> 0 us
  other arithmetic: 2.63 us -> 0 us
    pallas_call x0 -> x1, Pallas kernels: none -> 69.8 us  [body(): pl.pallas_call(functools.partial(kernel, dims), out_shape=jax.ShapeDtypeS...]
    unnamed x3 -> x0, waiting for transfers between devices: 68.6 us -> none
    all_to_all x4 -> x0, blocking collectives: 49.1 us -> none  [the longest x1 19 us: body(): lax.all_to_all(outgoing, 'lang', split_axis=0, concat_axis=0, tiled=True)]
    all_gather x1 -> x0, waiting for transfers between devices: 26.1 us -> none  [body(): halves = lax.all_gather(panels, 'mp', axis=2, tiled=True)]
    dot_general x10 -> x0, matrix products: 21.8 us -> none  [the longest x1 4.64 us: back_project(): lax.dot_general(flat_keys, key_cols, contract, preferred_element_type=jnp...]
    convert_element_type x4 -> x0, local copies, waits for them, and re-layouts: 7.44 us -> none  [the longest x2 6.44 us: body(): term.astype(jnp.bfloat16)]
    unnamed x21 -> x1, local copies, waits for them, and re-layouts: 6.81 us -> 1.67 us
    all_to_all x1 -> x0, starting transfers between devices: 3.22 us -> none  [body(): lax.all_to_all(sent_len, 'lang', split_axis=0, concat_axis=0, tiled=True)]
  transfers between devices with their start and end apart: 3 -> 0, of which waited for: 3 -> 0; matrix products, arithmetic and copies ran while one was open for 2% -> 0% of each run, Pallas kernels for 0% -> 0%
where the time goes in v1:
time: 71.6 us; the launch traced here: 71.5 us
  Pallas kernels  69.8 us (97%)
  local copies, waits for them, and re-layouts  1.67 us (2%)
    pallas_call x1, Pallas kernels, body(): pl.pallas_call(functools.partial(kernel, dims), out_shape=jax.ShapeDtypeS...  69.8 us
    unnamed x1, local copies, waits for them, and re-layouts  1.67 us

profile of v1, /device:TPU:1, one launch (start us, length us, event | category | flops | bytes accessed | tf_op | source)
XLA Modules:
  0.0 71.5 jit_solution(14484739538040378878)
XLA Ops:
  0.0 69.8 %shard_map.82 = bf16[1,2,128,512]{3,2,1,0:T(8,128)(2,1)} custom-call(s32[1,4]{1,0:T(1,128)} %lang_rows.1, s32[4]{0:T(128)} %group_of_lang.1, s32[1,2]{1,0:T(1,128)} %src_len.1, bf16[1,2,128,512]{3,2,1,0:T(8,128)(2,1)} %memory.1, bf16[1,2,128,768]{3,2,1,0:T(8,128)(2,1)} %queries_hbm.1, bf16[1,2,128,768]{3,2,1,0:T(8,128)(2,1)} %grads_hbm.1, ...), custom_call_target="tpu_custom_call" | custom-call | tf_op jit(solution)/shard_map/pallas_call | solution.py:397
  69.8 1.7 %copy.10 = bf16[1,2,128,512]{3,2,1,0:T(8,128)(2,1)} copy(bf16[1,2,128,512]{3,2,1,0:T(8,128)(2,1)} %shard_map.82) | data formatting | bytes 524288

commit v2 on v1

--- a/solution.py
+++ b/solution.py
@@ -17,7 +17,7 @@
     lang_rows,
     group_of_lang,
     src_len,
-    memory,
+    memory_hbm,
     queries_hbm,
     grads_hbm,
     key_hbm,
@@ -25,6 +25,7 @@
     out,
     key_w,
     value_w,
+    memory,
     query_v,
     grad_v,
     outgoing,
@@ -62,6 +63,8 @@
         pltpu.make_async_copy(grads_hbm.at[0], grad_v, load_sem.at[3]),
     ]
 
+    fetch = pltpu.make_async_copy(memory_hbm, memory, load_sem.at[4])
+    fetch.start()
     barrier = pltpu.get_barrier_semaphore()
     for ds in range(sectors):
         for dl in range(groups):
@@ -82,6 +85,7 @@
     home = lax.div(ml, half)
     slot = lax.rem(ml, half)
     at_home = home == ms
+    fetch.wait()
     for dl in range(groups):
         g = lax.rem(ml + dl, groups)
         index, routed = 0, 0
@@ -139,6 +143,20 @@
         for copy in z_copy(dl):
             copy.start()
 
+    relay = quarters == 4
+
+    def peer(dq):
+        if not relay:
+            return lax.rem(mq + dq, quarters)
+        near = mq + 1 - 2 * lax.rem(mq, 2)
+        far = mq + 2 - 4 * lax.div(mq, 2)
+        if isinstance(dq, int):
+            return (mq, near, far, 3 - mq)[dq]
+        return jnp.where(dq == 0, mq, jnp.where(dq == 1, near, jnp.where(dq == 2, far, 3 - mq)))
+
+    def first_axis(s):
+        return 1 + s % 2 if isinstance(s, int) else 1 + lax.rem(s, 2)
+
     def landed(s, q, ls):
         view = rows.at[s, q, ls]
         pltpu.make_async_copy(view, view, rows_recv.at[s, q, ls]).wait()
@@ -149,76 +167,75 @@
             dst_ref=rows.at[s, mq, ls],
             send_sem=mp_send.at[dq - 1, s, ls],
             recv_sem=rows_recv.at[s, mq, ls],
-            device_id=(ms, ml, lax.rem(mq + dq, quarters)),
+            device_id=(ms, ml, peer(dq)),
+            device_id_type=MESH,
+        )
+
+    def relay_copy(s, ls):
+        q = peer(3 - first_axis(s))
+        return pltpu.make_async_remote_copy(
+            src_ref=rows.at[s, q, ls],
+            dst_ref=rows.at[s, q, ls],
+            send_sem=mp_send.at[2, s, ls],
+            recv_sem=rows_recv.at[s, q, ls],
+            device_id=(ms, ml, peer(first_axis(s))),
             device_id_type=MESH,
         )
 
     nearest = jnp.clip(ml - ms * half, 0, half - 1)
 
-    def forward(i, carry):
-        ls = lax.rem(nearest + lax.div(i, sectors), half)
-        s = lax.rem(i, sectors)
-        landed(s, mq, ls)
-        for dq in range(quarters - 1, 0, -1):
-            mp_copy(s, ls, dq).start()
-        return carry
-
-    lax.fori_loop(0, sectors * half, forward, 0)
-
-    pair = 2 if half % 2 == 0 else 1
-    tall = pair * source
-    acc_k[...] = jnp.zeros_like(acc_k)
-    acc_v[...] = jnp.zeros_like(acc_v)
-    for load in loads:
-        load.wait()
-
-    def project(i, carry):
-        q = lax.rem(mq + lax.div(i, sectors), quarters)
-        s = lax.rem(i, sectors)
-
-        @pl.when(q != mq)
-        def _():
-            def wait_slot(ls, c):
+    def slot_of(k):
+        return lax.rem(nearest + k, half)
+
+    spread = (2, 1) if relay else tuple(range(quarters - 1, 0, -1))
+
+    def gather(ls):
+        for s in range(sectors):
+            landed(s, mq, ls)
+            for dq in spread:
+                mp_copy(s, ls, dq).start()
+
+    def pass_on(ls):
+        if relay:
+            for s in range(sectors):
+                landed(s, peer(3 - first_axis(s)), ls)
+                relay_copy(s, ls).start()
+
+    def project(ls):
+        acc_k[...] = jnp.zeros_like(acc_k)
+        acc_v[...] = jnp.zeros_like(acc_v)
+
+        def step(i, carry):
+            dq, s = lax.div(i, sectors), lax.rem(i, sectors)
+            q = peer(dq)
+            fresh = dq > 0
+            if relay:
+                fresh = jnp.logical_and(fresh, dq != 3 - first_axis(s))
+
+            @pl.when(fresh)
+            def _():
                 landed(s, q, ls)
-                return c
-
-            lax.fori_loop(0, half, wait_slot, 0)
-
-        start = pl.multiple_of((s * quarters + q) * eighth, eighth)
-
-        def chunk(m, c):
-            x = rows[s, q, pl.ds(m * pair, pair)].reshape(tall, eighth)
-            at = pl.ds(pl.multiple_of(m * tall, tall), tall)
-            acc_k[at, :] += jnp.dot(
-                x, key_w[pl.ds(start, eighth), :], preferred_element_type=jnp.float32
-            )
-            acc_v[at, :] += jnp.dot(
-                x, value_w[pl.ds(start, eighth), :], preferred_element_type=jnp.float32
-            )
-            return c
-
-        return lax.fori_loop(0, half // pair, chunk, carry)
-
-    lax.fori_loop(0, sectors * quarters, project, 0)
-
-    def wait_len(i, carry):
-        ls, s = lax.div(i, sectors), lax.rem(i, sectors)
-        view = got_len.at[ls, s]
-        pltpu.make_async_copy(view, view, len_recv.at[ls, s]).wait()
-        return carry
-
-    lax.fori_loop(0, sectors * half, wait_len, 0)
+
+            at = pl.ds(pl.multiple_of((s * quarters + q) * eighth, eighth), eighth)
+            x = rows[s, q, ls]
+            acc_k[...] += jnp.dot(x, key_w[at, :], preferred_element_type=jnp.float32)
+            acc_v[...] += jnp.dot(x, value_w[at, :], preferred_element_type=jnp.float32)
+            return carry
+
+        lax.fori_loop(0, sectors * quarters, step, 0)
 
     scaling = HD ** (-0.5)
     position = lax.broadcasted_iota(jnp.int32, (source, query_v.shape[1]), 0)
 
-    def attend(ls, carry):
-        at = pl.ds(pl.multiple_of(ls * source, source), source)
+    def attend(ls):
+        for s in range(sectors):
+            view = got_len.at[ls, s]
+            pltpu.make_async_copy(view, view, len_recv.at[ls, s]).wait()
         visible = position < got_len[ls, 0][0:1, :]
         for h in range(heads_w // HD):
             cols = slice(h * HD, (h + 1) * HD)
-            k = acc_k[at, cols].astype(jnp.bfloat16)
-            v = acc_v[at, cols].astype(jnp.bfloat16)
+            k = acc_k[:, cols].astype(jnp.bfloat16)
+            v = acc_v[:, cols].astype(jnp.bfloat16)
             q = query_v[ls, :, cols]
             d = grad_v[ls, :, cols]
             scores = lax.dot_general(k, q, NT, preferred_element_type=jnp.float32) * scaling
@@ -227,61 +244,72 @@
             grad_probs = lax.dot_general(v, d, NT, preferred_element_type=jnp.float32)
             deltas = jnp.sum(probs * grad_probs, axis=0, keepdims=True)
             grad_scores = (probs * (grad_probs - deltas) * scaling).astype(jnp.bfloat16)
-            key_rows[at, cols] = jnp.dot(
+            key_rows[:, cols] = jnp.dot(
                 grad_scores, q, preferred_element_type=jnp.float32
             ).astype(jnp.bfloat16)
-            value_rows[at, cols] = jnp.dot(
+            value_rows[:, cols] = jnp.dot(
                 probs.astype(jnp.bfloat16), d, preferred_element_type=jnp.float32
             ).astype(jnp.bfloat16)
-        return carry
-
-    lax.fori_loop(0, half, attend, 0)
 
     def part_copy(s, ls, dq):
-        q = lax.rem(mq + dq, quarters)
+        to = peer(dq)
+        if relay:
+            if isinstance(dq, int):
+                to = peer(first_axis(s)) if dq == 3 else to
+            else:
+                to = jnp.where(dq == 3, peer(first_axis(s)), to)
         return pltpu.make_async_remote_copy(
             src_ref=part.at[dq - 1, s, ls],
             dst_ref=inbox.at[dq - 1, s, ls],
             send_sem=part_send.at[dq - 1, s, ls],
             recv_sem=part_recv.at[dq - 1, s, ls],
-            device_id=(ms, ml, q),
-            device_id_type=MESH,
-        )
-
-    def project_back(s, q, m):
-        start = pl.multiple_of((s * quarters + q) * eighth, eighth)
-        at = pl.ds(pl.multiple_of(m * tall, tall), tall)
+            device_id=(ms, ml, to),
+            device_id_type=MESH,
+        )
+
+    def project_back(s, q):
+        at = pl.ds(pl.multiple_of((s * quarters + q) * eighth, eighth), eighth)
         term = lax.dot_general(
-            key_rows[at, :], key_w[pl.ds(start, eighth), :], NT,
-            preferred_element_type=jnp.float32,
+            key_rows[...], key_w[at, :], NT, preferred_element_type=jnp.float32
         )
         return term + lax.dot_general(
-            value_rows[at, :], value_w[pl.ds(start, eighth), :], NT,
-            preferred_element_type=jnp.float32,
-        )
-
-    chunks = half // pair
-
-    def send_part(i, carry):
-        m = lax.rem(i, chunks)
-        s = lax.rem(lax.div(i, chunks), sectors)
-        dq = quarters - 1 - lax.div(i, chunks * sectors)
-        term = project_back(s, lax.rem(mq + dq, quarters), m)
-        part[dq - 1, s, pl.ds(m * pair, pair)] = term.astype(jnp.bfloat16).reshape(
-            pair, source, eighth
-        )
-        for p in range(pair):
-            part_copy(s, m * pair + p, dq).start()
-        return carry
-
-    lax.fori_loop(0, (quarters - 1) * sectors * chunks, send_part, 0)
-
-    def keep_part(i, carry):
-        m, s = lax.rem(i, chunks), lax.div(i, chunks)
-        own[s, pl.ds(m * pair, pair)] = project_back(s, mq, m).reshape(pair, source, eighth)
-        return carry
-
-    lax.fori_loop(0, sectors * chunks, keep_part, 0)
+            value_rows[...], value_w[at, :], NT, preferred_element_type=jnp.float32
+        )
+
+    held = 1 if relay else 0
+
+    def backward(ls):
+        def send(i, carry):
+            step, s = lax.div(i, sectors), lax.rem(i, sectors)
+            dq = quarters - 1 - step
+            if relay:
+                dq = jnp.where(step == 0, 3, first_axis(s))
+            part[dq - 1, s, ls] = project_back(s, peer(dq)).astype(jnp.bfloat16)
+            part_copy(s, ls, dq).start()
+            return carry
+
+        lax.fori_loop(0, sectors * (quarters - 1 - held), send, 0)
+
+        def keep(i, carry):
+            step, s = lax.div(i, sectors), lax.rem(i, sectors)
+            dq = jnp.where(step == 0, 3 - first_axis(s), 0) if relay else 0
+            own[held - step, s, ls] = project_back(s, peer(dq))
+            return carry
+
+        lax.fori_loop(0, sectors * (1 + held), keep, 0)
+
+    def part_landed(s, ls, dq):
+        view = inbox.at[dq - 1, s, ls]
+        pltpu.make_async_copy(view, view, part_recv.at[dq - 1, s, ls]).wait()
+        return inbox[dq - 1, s, ls].astype(jnp.float32)
+
+    def sum_on(ls):
+        if relay:
+            for s in range(sectors):
+                dq = 3 - first_axis(s)
+                total = own[1, s, ls] + part_landed(s, ls, 3)
+                part[dq - 1, s, ls] = total.astype(jnp.bfloat16)
+                part_copy(s, ls, dq).start()
 
     def back_copy(s, ls):
         return pltpu.make_async_remote_copy(
@@ -299,26 +327,44 @@
     def is_me(s, ls):
         return jnp.logical_and(s == ms, ms * half + ls == ml)
 
-    def reduce(i, carry):
-        ls, s = lax.rem(i, half), lax.div(i, half)
-        total = own[s, ls]
-        for dq in range(quarters - 1, 0, -1):
-            view = inbox.at[dq - 1, s, ls]
-            pltpu.make_async_copy(view, view, part_recv.at[dq - 1, s, ls]).wait()
-            total = total + inbox[dq - 1, s, ls].astype(jnp.float32)
-        reduced[s, ls] = total.astype(jnp.bfloat16)
-
-        @pl.when(is_me(s, ls))
-        def _():
-            local_back(s, ls).start()
-
-        @pl.when(jnp.logical_not(is_me(s, ls)))
-        def _():
-            back_copy(s, ls).start()
-
-        return carry
-
-    lax.fori_loop(0, sectors * half, reduce, 0)
+    def give_back(ls):
+        for s in range(sectors):
+            total = own[0, s, ls]
+            if relay:
+                total = total + part_landed(s, ls, first_axis(s))
+                total = total + part_landed(s, ls, 3 - first_axis(s))
+            else:
+                for dq in range(1, quarters):
+                    total = total + part_landed(s, ls, dq)
+            reduced[s, ls] = total.astype(jnp.bfloat16)
+
+            @pl.when(is_me(s, ls))
+            def _():
+                local_back(s, ls).start()
+
+            @pl.when(jnp.logical_not(is_me(s, ls)))
+            def _():
+                back_copy(s, ls).start()
+
+    gather(slot_of(0))
+    pass_on(slot_of(0))
+    for k in range(half):
+        if k + 1 < half:
+            gather(slot_of(k + 1))
+        if k == 0:
+            for load in loads:
+                load.wait()
+        project(slot_of(k))
+        if k + 1 < half:
+            pass_on(slot_of(k + 1))
+        attend(slot_of(k))
+        if k > 0:
+            sum_on(slot_of(k - 1))
+        backward(slot_of(k))
+        if k > 0:
+            give_back(slot_of(k - 1))
+    sum_on(slot_of(half - 1))
+    give_back(slot_of(half - 1))
 
     for g in range(groups):
         view = arrived.at[g]
@@ -368,22 +414,23 @@
     scratch = [
         pltpu.VMEM((width, heads_w), low),
         pltpu.VMEM((width, heads_w), low),
+        pltpu.VMEM(memory.shape, low),
         pltpu.VMEM(queries.shape[1:], low),
         pltpu.VMEM(queries.shape[1:], low),
         pltpu.VMEM((groups, source, eighth), low),
         pltpu.VMEM((groups, 8, queries.shape[2]), jnp.int32),
         pltpu.VMEM((half, sectors, 8, queries.shape[2]), jnp.int32),
         pltpu.VMEM((sectors, quarters, half, source, eighth), low),
-        pltpu.VMEM((half * source, heads_w), full),
-        pltpu.VMEM((half * source, heads_w), full),
-        pltpu.VMEM((half * source, heads_w), low),
-        pltpu.VMEM((half * source, heads_w), low),
+        pltpu.VMEM((source, heads_w), full),
+        pltpu.VMEM((source, heads_w), full),
+        pltpu.VMEM((source, heads_w), low),
+        pltpu.VMEM((source, heads_w), low),
         pltpu.VMEM((quarters - 1, sectors, half, source, eighth), low),
-        pltpu.VMEM((sectors, half, source, eighth), full),
+        pltpu.VMEM((2, sectors, half, source, eighth), full),
         pltpu.VMEM((quarters - 1, sectors, half, source, eighth), low),
         pltpu.VMEM((sectors, half, source, eighth), low),
         pltpu.VMEM((groups, source, eighth), low),
-        dma((4,)),
+        dma((5,)),
         dma((groups,)),
         dma((groups,)),
         dma((half, sectors)),
@@ -397,7 +444,7 @@
     return pl.pallas_call(
         functools.partial(kernel, dims),
         out_shape=jax.ShapeDtypeStruct(memory.shape, memory.dtype),
-        in_specs=[smem, smem, smem, vmem, hbm, hbm, hbm, hbm],
+        in_specs=[smem, smem, smem, hbm, hbm, hbm, hbm, hbm],
         out_specs=vmem,
         scratch_shapes=scratch,
         compiler_params=pltpu.CompilerParams(

time: 71.6 us -> 64.1 us (0.90)
  Pallas kernels: 69.8 us -> 62.3 us
    pallas_call x1, Pallas kernels: 69.8 us -> 62.3 us  [body(): pl.pallas_call(functools.partial(kernel, dims), out_shape=jax.ShapeDtypeS...]
where the time goes in v2:
time: 64.1 us; the launch traced here: 63.9 us
  Pallas kernels  62.3 us (97%)
  local copies, waits for them, and re-layouts  1.67 us (3%)
    pallas_call x1, Pallas kernels, body(): pl.pallas_call(functools.partial(kernel, dims), out_shape=jax.ShapeDtypeS...  62.3 us
    unnamed x1, local copies, waits for them, and re-layouts  1.67 us

profile of v2, /device:TPU:1, one launch (start us, length us, event | category | flops | bytes accessed | tf_op | source)
XLA Modules:
  0.0 63.9 jit_solution(12675161715669618751)
XLA Ops:
  0.0 62.3 %shard_map.82 = bf16[1,2,128,512]{3,2,1,0:T(8,128)(2,1)} custom-call(s32[1,4]{1,0:T(1,128)} %lang_rows.1, s32[4]{0:T(128)} %group_of_lang.1, s32[1,2]{1,0:T(1,128)} %src_len.1, bf16[1,2,128,512]{3,2,1,0:T(8,128)(2,1)} %memory_hbm.1, bf16[1,2,128,768]{3,2,1,0:T(8,128)(2,1)} %queries_hbm.1, bf16[1,2,128,768]{3,2,1,0:T(8,128)(2,1)} %grads_hbm.1, ...), custom_call_target="tpu_custom_call" | custom-call | tf_op jit(solution)/shard_map/pallas_call | solution.py:444
  62.3 1.7 %copy.10 = bf16[1,2,128,512]{3,2,1,0:T(8,128)(2,1)} copy(bf16[1,2,128,512]{3,2,1,0:T(8,128)(2,1)} %shard_map.82) | data formatting | bytes 524288

commit v3 on v2

--- a/solution.py
+++ b/solution.py
@@ -189,17 +189,15 @@
 
     spread = (2, 1) if relay else tuple(range(quarters - 1, 0, -1))
 
-    def gather(ls):
-        for s in range(sectors):
-            landed(s, mq, ls)
-            for dq in spread:
-                mp_copy(s, ls, dq).start()
-
-    def pass_on(ls):
+    def gather(ls, s):
+        landed(s, mq, ls)
+        for dq in spread:
+            mp_copy(s, ls, dq).start()
+
+    def pass_on(ls, s):
         if relay:
-            for s in range(sectors):
-                landed(s, peer(3 - first_axis(s)), ls)
-                relay_copy(s, ls).start()
+            landed(s, peer(3 - first_axis(s)), ls)
+            relay_copy(s, ls).start()
 
     def project(ls):
         acc_k[...] = jnp.zeros_like(acc_k)
@@ -346,18 +344,22 @@
             def _():
                 back_copy(s, ls).start()
 
-    gather(slot_of(0))
-    pass_on(slot_of(0))
+    for s in range(sectors):
+        gather(slot_of(0), s)
     for k in range(half):
-        if k + 1 < half:
-            gather(slot_of(k + 1))
+        for s in range(sectors):
+            if k == 0:
+                pass_on(slot_of(k), s)
+            if k + 1 < half:
+                gather(slot_of(k + 1), s)
         if k == 0:
             for load in loads:
                 load.wait()
         project(slot_of(k))
+        attend(slot_of(k))
         if k + 1 < half:
-            pass_on(slot_of(k + 1))
-        attend(slot_of(k))
+            for s in range(sectors):
+                pass_on(slot_of(k + 1), s)
         if k > 0:
             sum_on(slot_of(k - 1))
         backward(slot_of(k))

time: 64.1 us -> 63.1 us (0.984)
  Pallas kernels: 62.3 us -> 61.3 us
    pallas_call x1, Pallas kernels: 62.3 us -> 61.3 us  [body(): pl.pallas_call(functools.partial(kernel, dims), out_shape=jax.ShapeDtypeS...]
where the time goes in v3:
time: 63.1 us; the launch traced here: 63 us
  Pallas kernels  61.3 us (97%)
  local copies, waits for them, and re-layouts  1.67 us (3%)
    pallas_call x1, Pallas kernels, body(): pl.pallas_call(functools.partial(kernel, dims), out_shape=jax.ShapeDtypeS...  61.3 us
    unnamed x1, local copies, waits for them, and re-layouts  1.67 us

profile of v3, /device:TPU:1, one launch (start us, length us, event | category | flops | bytes accessed | tf_op | source)
XLA Modules:
  0.0 63.0 jit_solution(10714997360995660921)
XLA Ops:
  0.0 61.3 %shard_map.82 = bf16[1,2,128,512]{3,2,1,0:T(8,128)(2,1)} custom-call(s32[1,4]{1,0:T(1,128)} %lang_rows.1, s32[4]{0:T(128)} %group_of_lang.1, s32[1,2]{1,0:T(1,128)} %src_len.1, bf16[1,2,128,512]{3,2,1,0:T(8,128)(2,1)} %memory_hbm.1, bf16[1,2,128,768]{3,2,1,0:T(8,128)(2,1)} %queries_hbm.1, bf16[1,2,128,768]{3,2,1,0:T(8,128)(2,1)} %grads_hbm.1, ...), custom_call_target="tpu_custom_call" | custom-call | tf_op jit(solution)/shard_map/pallas_call | solution.py:446
  61.3 1.7 %copy.10 = bf16[1,2,128,512]{3,2,1,0:T(8,128)(2,1)} copy(bf16[1,2,128,512]{3,2,1,0:T(8,128)(2,1)} %shard_map.82) | data formatting | bytes 524288
